TPU v7x, 32 devices: a whole 2x2x4 slice. The times are simulated.
32 devices in a mesh: seg: 4 (over y, x), slab: 8 (over z, core).
Axes of the slice: x: 2, y: 2, z: 4, core: 2. Of those that a mesh axis runs over, the one named last changes fastest.
Arguments:
- positions: bfloat16 [4, 32, 3, 642], P('seg', 'slab'), may hold values from -6 to 6
- density: bfloat16 [4, 32, 3, 642], P('seg', 'slab'), may hold values from -6 to 6
- upsample: bfloat16 [642, 2562], replicated, may hold values from -0.25 to 0.25
- quad_weights: float32 [2562], replicated, may hold values from 0.3 to 3
- coarse_weights: float32 [642], replicated, may hold values from 0.3 to 3
- pair_target: int32 [4, 16], P('seg', 'slab'), may hold values from 0 to 3
- pair_source: int32 [4, 16], P('seg', 'slab'), may hold values from 0 to 7
- junction_cell: int32 [4, 8, 4], P('seg', 'slab'), may hold values from 0 to 3
- junction_target: int32 [4, 8, 4], P('seg', 'slab'), may hold values from 0 to 3
- wall_points: bfloat16 [4, 8, 3, 128], P('seg', 'slab'), may hold values from -6 to 6
- wall_traction: bfloat16 [4, 8, 3, 128], P('seg', 'slab'), may hold values from -6 to 6
- wall_near: int32 [4, 32, 2], P('seg', 'slab'), may hold values from 0 to 7
Outputs:
- velocity: float32 [4, 32, 3, 642], P('seg', 'slab')
All inputs are finite; a program needn't handle non-finite values.
Results may differ from a plain program's by a relative error of at most 0.0024.
Values may be sent and summed in bfloat16 or wider, within the bound.
A program may use at most 64 MiB of HBM per device.

v0:
```python
import math
import jax
import jax.numpy as jnp
from jax import lax
from jax.sharding import PartitionSpec as P

HALO = 2
EPSILON2 = 0.05
WALL_GAIN = 3.0


def with_halo(block, sides, width):
    for axis, dim in sides:
        count = lax.axis_size(axis)
        forward = [(i, i + 1) for i in range(count - 1)]
        backward = [(target, source) for source, target in forward]
        low = lax.ppermute(
            lax.slice_in_dim(block, block.shape[dim] - width, None, axis=dim), axis, forward
        )
        high = lax.ppermute(lax.slice_in_dim(block, 0, width, axis=dim), axis, backward)
        block = jnp.concatenate([low, block, high], axis=dim)
    return block


def kernel_rows(targets, sources, strength):
    offset = targets[:, :, None] - sources[:, None, :]
    distance2 = jnp.sum(offset * offset, axis=0)
    inverse = lax.rsqrt(distance2 + EPSILON2)
    inverse3 = inverse * inverse * inverse
    along_offset = jnp.sum(offset * strength[:, None, :], axis=0)
    summand = (
        strength[:, None, :] * (distance2 + 2.0 * EPSILON2) + along_offset[None] * offset
    ) * inverse3[None]
    return jnp.sum(summand, axis=2) / (8.0 * math.pi)


def stokes_block(targets, sources, strength):
    points = targets.shape[1]
    blocked = targets.reshape(3, 6, points // 6).transpose(1, 0, 2)
    result = lax.map(lambda target_rows: kernel_rows(target_rows, sources, strength), blocked)
    return result.transpose(1, 0, 2).reshape(3, points)


def add_to_cells(blocks, index, cell_count):
    onehot = (index[None, :] == jnp.arange(cell_count, dtype=jnp.int32)[:, None]).astype(
        jnp.float32
    )
    return jnp.einsum("cn,nkp->ckp", onehot, blocks, precision=lax.Precision.HIGHEST)


def local(
    positions,
    density,
    upsample,
    quad_weights,
    coarse_weights,
    pair_target,
    pair_source,
    junction_cell,
    junction_target,
    wall_points,
    wall_traction,
    wall_near,
):
    coarse_pos = positions[0]
    coarse_den = density[0]
    cell_count = coarse_pos.shape[0]
    rim_pos, rim_den = (
        with_halo(coarse_pos, (("slab", 0),), HALO),
        with_halo(coarse_den, (("slab", 0),), HALO),
    )
    fine_pos = jnp.einsum(
        "ckp,pq->ckq", rim_pos, upsample, preferred_element_type=jnp.float32
    ).astype(jnp.bfloat16)
    fine_den = jnp.einsum(
        "ckp,pq->ckq", rim_den, upsample, preferred_element_type=jnp.float32
    ).astype(jnp.bfloat16)
    targets = pair_target[0]
    sources = pair_source[0]

    def fine_pair(operands):
        target_pts, source_pts, source_den = operands
        strength = source_den.astype(jnp.float32) * quad_weights[None, :]
        return stokes_block(
            target_pts.astype(jnp.float32), source_pts.astype(jnp.float32), strength
        )

    local_blocks = lax.map(fine_pair, (coarse_pos[targets], fine_pos[sources], fine_den[sources]))
    velocity = add_to_cells(local_blocks, targets, cell_count)
    chosen = junction_cell[0, 0]
    arrived_pos, arrived_den = (
        lax.all_to_all(coarse_pos[chosen], "seg", split_axis=0, concat_axis=0, tiled=True),
        lax.all_to_all(coarse_den[chosen], "seg", split_axis=0, concat_axis=0, tiled=True),
    )
    goals = junction_target[0, 0]
    alive_mask = (jnp.arange(goals.shape[0], dtype=jnp.int32) != lax.axis_index("seg")).astype(
        jnp.float32
    )

    def coarse_pair(operands):
        target_pts, source_pts, source_den = operands
        strength = source_den.astype(jnp.float32) * coarse_weights[None, :]
        return stokes_block(
            target_pts.astype(jnp.float32), source_pts.astype(jnp.float32), strength
        )

    junction_blocks = (
        lax.map(coarse_pair, (coarse_pos[goals], arrived_pos, arrived_den))
        * alive_mask[:, None, None]
    )
    velocity = velocity + add_to_cells(junction_blocks, goals, cell_count)
    patch_pos, patch_trac = (
        lax.all_gather(wall_points[0], "slab", axis=0, tiled=True),
        lax.all_gather(wall_traction[0], "slab", axis=0, tiled=True),
    )
    near_rows = wall_near[0].reshape(-1)
    near_count = wall_near.shape[2]

    def wall_pair(operands):
        target_pts, source_pts, source_den = operands
        return stokes_block(
            target_pts.astype(jnp.float32),
            source_pts.astype(jnp.float32),
            source_den.astype(jnp.float32) * WALL_GAIN,
        )

    wall_blocks = lax.map(
        wall_pair,
        (jnp.repeat(coarse_pos, near_count, axis=0), patch_pos[near_rows], patch_trac[near_rows]),
    )
    velocity = velocity + jnp.sum(
        wall_blocks.reshape((cell_count, near_count) + wall_blocks.shape[1:]), axis=1
    )
    return velocity[None]


def solution(mesh):
    placed = (
        P("seg", "slab", None, None),
        P("seg", "slab", None, None),
        P(),
        P(),
        P(),
        P("seg", "slab"),
        P("seg", "slab"),
        P("seg", "slab", None),
        P("seg", "slab", None),
        P("seg", "slab", None, None),
        P("seg", "slab", None, None),
        P("seg", "slab", None),
    )
    return jax.shard_map(
        local, mesh=mesh, in_specs=placed, out_specs=P("seg", "slab", None, None), check_vma=False
    )
```

profile of v0, /device:TPU:0, one launch (start us, length us, event | category | flops | bytes accessed | tf_op | source)
XLA Modules:
  0.0 205.6 jit_solution(8631033830005076879)
XLA Ops:
  1.5 3.0 %collective-permute-start = (bf16[2,3,642]{2,0,1:T(2,128)(2,1)}, bf16[2,3,642]{2,0,1:T(2,128)(2,1)}, u32[]{:S(2)}, u32[]{:S(2)}) collective-permute-start(bf16[2,3,642]{2,0,1:T(2,128)(2,1)} %get-tuple-element.324), channel_id=1, source_target_pairs={{0,1},{1,2},{2,3},{3,4},{4,5},{5,6},{6,7},{8,9},{9,10},{10,11},{11... | collective-permute-start | bytes 23120 | tf_op jit(solution)/shard_map/ppermute | solution.py:17
  7.2 5.2 %collective-permute-start.2 = (bf16[2,3,642]{2,0,1:T(2,128)(2,1)}, bf16[2,3,642]{2,0,1:T(2,128)(2,1)}, u32[]{:S(2)}, u32[]{:S(2)}) collective-permute-start(bf16[2,3,642]{2,0,1:T(2,128)(2,1)} %get-tuple-element.322), channel_id=1, source_target_pairs={{0,1},{1,2},{2,3},{3,4},{4,5},{5,6},{6,7},{8,9},{9,10},{10,11},{11... | collective-permute-start | bytes 23120 | tf_op jit(solution)/shard_map/ppermute | solution.py:17
  16.3 3.9 %all-to-all-start = ((bf16[4,3,642]{2,1,0:T(4,128)(2,1)}), bf16[4,3,642]{2,1,0:T(4,128)(2,1)}, u32[]{:S(2)}, u32[]{:S(2)}) async-start(bf16[4,3,642]{2,1,0:T(4,128)(2,1)} %gather_fusion.4), calls=%async_computation | async-start | bytes 49152 | tf_op jit(solution)/shard_map/all_to_all | solution.py:92
  24.8 14.1 %all-gather = bf16[8,1,3,128]{3,2,1,0:T(4,128)(2,1)S(1)} all-gather(bf16[1,1,3,128]{3,2,1,0:T(4,128)(2,1)} %param.33), channel_id=2, replica_groups=mesh['seg'=4,'slab'=8] {'slab'}, dimensions={0}, use_global_device_ids=true | all-gather | bytes 6912 | tf_op jit(solution)/shard_map/all_gather | solution.py:113
  38.9 9.0 %all-gather.1 = bf16[8,1,3,128]{3,2,1,0:T(4,128)(2,1)S(1)} all-gather(bf16[1,1,3,128]{3,2,1,0:T(4,128)(2,1)} %param.34), channel_id=3, replica_groups=mesh['seg'=4,'slab'=8] {'slab'}, dimensions={0}, use_global_device_ids=true | all-gather | bytes 6912 | tf_op jit(solution)/shard_map/all_gather | solution.py:114
  50.2 37.8 %while.65 = (s32[]{:T(128)}, f32[8,3,642]{2,1,0:T(4,128)}, bf16[8,3,642]{2,1,0:T(4,128)(2,1)}, bf16[8,3,128]{2,1,0:T(4,128)(2,1)S(1)}, bf16[8,3,128]{2,1,0:T(4,128)(2,1)}, /*index=5*/s32[]{:T(128)}, s32[]{:T(128)}, s32[]{:T(128)}) while((s32[]{:T(128)}, f32[8,3,642]{2,1,0:T(4,128)}, bf16[8,3,642]{2,1,0:T(4,128)(2,1)}, ...), condition=%wide.region_20.21_spmd, body=%wide.region_14.20_spmd.sunk | while | flops 482442 | bytes 540622 | solution.py:127
  51.6 2.6 %while.68 = (s32[]{:T(128)}, f32[6,3,107]{2,1,0:T(4,128)S(1)}, f32[3,128]{1,0:T(4,128)S(1)}, f32[6,3,107]{2,0,1:T(8,128)S(1)}, f32[3,128]{1,0:T(4,128)S(1)}, /*index=5*/s32[]{:T(128)}) while((s32[]{:T(128)}, f32[6,3,107]{2,1,0:T(4,128)S(1)}, f32[3,128]{1,0:T(4,128)S(1)}, f32[6,3,107]{2,0,1:T(8,128)S(1)}, f32[3,128]{1,0:T(4,128)S(1)}, ...), condition=%wide.region_19.19_spmd, body=%wide.region_15.18_spmd.sunk | while | flops 479362 | bytes 457577 | solution.py:40
  56.4 2.6 %while.68 = (s32[]{:T(128)}, f32[6,3,107]{2,1,0:T(4,128)S(1)}, f32[3,128]{1,0:T(4,128)S(1)}, f32[6,3,107]{2,0,1:T(8,128)S(1)}, f32[3,128]{1,0:T(4,128)S(1)}, /*index=5*/s32[]{:T(128)}) while((s32[]{:T(128)}, f32[6,3,107]{2,1,0:T(4,128)S(1)}, f32[3,128]{1,0:T(4,128)S(1)}, f32[6,3,107]{2,0,1:T(8,128)S(1)}, f32[3,128]{1,0:T(4,128)S(1)}, ...), condition=%wide.region_19.19_spmd, body=%wide.region_15.18_spmd.sunk | while | flops 479362 | bytes 457577 | solution.py:40
  61.1 2.6 %while.68 = (s32[]{:T(128)}, f32[6,3,107]{2,1,0:T(4,128)S(1)}, f32[3,128]{1,0:T(4,128)S(1)}, f32[6,3,107]{2,0,1:T(8,128)S(1)}, f32[3,128]{1,0:T(4,128)S(1)}, /*index=5*/s32[]{:T(128)}) while((s32[]{:T(128)}, f32[6,3,107]{2,1,0:T(4,128)S(1)}, f32[3,128]{1,0:T(4,128)S(1)}, f32[6,3,107]{2,0,1:T(8,128)S(1)}, f32[3,128]{1,0:T(4,128)S(1)}, ...), condition=%wide.region_19.19_spmd, body=%wide.region_15.18_spmd.sunk | while | flops 479362 | bytes 457577 | solution.py:40
  65.8 2.6 %while.68 = (s32[]{:T(128)}, f32[6,3,107]{2,1,0:T(4,128)S(1)}, f32[3,128]{1,0:T(4,128)S(1)}, f32[6,3,107]{2,0,1:T(8,128)S(1)}, f32[3,128]{1,0:T(4,128)S(1)}, /*index=5*/s32[]{:T(128)}) while((s32[]{:T(128)}, f32[6,3,107]{2,1,0:T(4,128)S(1)}, f32[3,128]{1,0:T(4,128)S(1)}, f32[6,3,107]{2,0,1:T(8,128)S(1)}, f32[3,128]{1,0:T(4,128)S(1)}, ...), condition=%wide.region_19.19_spmd, body=%wide.region_15.18_spmd.sunk | while | flops 479362 | bytes 457577 | solution.py:40
  70.6 2.6 %while.68 = (s32[]{:T(128)}, f32[6,3,107]{2,1,0:T(4,128)S(1)}, f32[3,128]{1,0:T(4,128)S(1)}, f32[6,3,107]{2,0,1:T(8,128)S(1)}, f32[3,128]{1,0:T(4,128)S(1)}, /*index=5*/s32[]{:T(128)}) while((s32[]{:T(128)}, f32[6,3,107]{2,1,0:T(4,128)S(1)}, f32[3,128]{1,0:T(4,128)S(1)}, f32[6,3,107]{2,0,1:T(8,128)S(1)}, f32[3,128]{1,0:T(4,128)S(1)}, ...), condition=%wide.region_19.19_spmd, body=%wide.region_15.18_spmd.sunk | while | flops 479362 | bytes 457577 | solution.py:40
  75.3 2.6 %while.68 = (s32[]{:T(128)}, f32[6,3,107]{2,1,0:T(4,128)S(1)}, f32[3,128]{1,0:T(4,128)S(1)}, f32[6,3,107]{2,0,1:T(8,128)S(1)}, f32[3,128]{1,0:T(4,128)S(1)}, /*index=5*/s32[]{:T(128)}) while((s32[]{:T(128)}, f32[6,3,107]{2,1,0:T(4,128)S(1)}, f32[3,128]{1,0:T(4,128)S(1)}, f32[6,3,107]{2,0,1:T(8,128)S(1)}, f32[3,128]{1,0:T(4,128)S(1)}, ...), condition=%wide.region_19.19_spmd, body=%wide.region_15.18_spmd.sunk | while | flops 479362 | bytes 457577 | solution.py:40
  80.0 2.6 %while.68 = (s32[]{:T(128)}, f32[6,3,107]{2,1,0:T(4,128)S(1)}, f32[3,128]{1,0:T(4,128)S(1)}, f32[6,3,107]{2,0,1:T(8,128)S(1)}, f32[3,128]{1,0:T(4,128)S(1)}, /*index=5*/s32[]{:T(128)}) while((s32[]{:T(128)}, f32[6,3,107]{2,1,0:T(4,128)S(1)}, f32[3,128]{1,0:T(4,128)S(1)}, f32[6,3,107]{2,0,1:T(8,128)S(1)}, f32[3,128]{1,0:T(4,128)S(1)}, ...), condition=%wide.region_19.19_spmd, body=%wide.region_15.18_spmd.sunk | while | flops 479362 | bytes 457577 | solution.py:40
  84.8 2.6 %while.68 = (s32[]{:T(128)}, f32[6,3,107]{2,1,0:T(4,128)S(1)}, f32[3,128]{1,0:T(4,128)S(1)}, f32[6,3,107]{2,0,1:T(8,128)S(1)}, f32[3,128]{1,0:T(4,128)S(1)}, /*index=5*/s32[]{:T(128)}) while((s32[]{:T(128)}, f32[6,3,107]{2,1,0:T(4,128)S(1)}, f32[3,128]{1,0:T(4,128)S(1)}, f32[6,3,107]{2,0,1:T(8,128)S(1)}, f32[3,128]{1,0:T(4,128)S(1)}, ...), condition=%wide.region_19.19_spmd, body=%wide.region_15.18_spmd.sunk | while | flops 479362 | bytes 457577 | solution.py:40
  98.9 2.2 %gather_fusion.1 = bf16[2,3,2562]{2,1,0:T(4,128)(2,1)} fusion(bf16[8,3,2562]{2,1,0:T(4,128)(2,1)} %copy.76, s32[1024]{0:T(1024)} %pad_clamp_fusion.3), kind=kCustom, calls=%fused_computation.1 | custom fusion | bytes 61496 | tf_op jit(solution)/shard_map/gather | solution.py:88
  101.2 2.2 %gather_fusion.2 = bf16[2,3,2562]{2,1,0:T(4,128)(2,1)} fusion(bf16[8,3,2562]{2,1,0:T(4,128)(2,1)} %copy.77, s32[1024]{0:T(1024)} %pad_clamp_fusion.3), kind=kCustom, calls=%fused_computation.2 | custom fusion | bytes 61496 | tf_op jit(solution)/shard_map/gather | solution.py:88
  103.4 47.6 %while.61 = (s32[]{:T(128)}, f32[2,3,642]{2,0,1:T(2,128)}, bf16[2,3,642]{2,1,0:T(4,128)(2,1)}, bf16[2,3,2562]{2,1,0:T(4,128)(2,1)}, bf16[2,3,2562]{2,1,0:T(4,128...) while((s32[]{:T(128)}, f32[2,3,642]{2,0,1:T(2,128)}, bf16[2,3,642]{2,1,0:T(4,128)(2,1)}, ...), condition=%wide.region_6.7_spmd, body=%wide.region_0.6_spmd.sunk | while | flops 9619678 | bytes 9207262 | solution.py:88
  106.3 19.4 %while.66 = (s32[]{:T(128)}, f32[6,3,107]{2,1,0:T(4,128)S(1)}, f32[3,2562]{1,0:T(4,128)S(1)}, f32[6,3,107]{2,0,1:T(8,128)S(1)}, f32[3,2562]{1,0:T(4,128)}, /*index=5*/s32[]{:T(128)}) while((s32[]{:T(128)}, f32[6,3,107]{2,1,0:T(4,128)S(1)}, f32[3,2562]{1,0:T(4,128)S(1)}, f32[6,3,107]{2,0,1:T(8,128)S(1)}, f32[3,2562]{1,0:T(4,128)}, ...), condition=%wide.region_5.5_spmd, body=%wide.region_1.4_spmd.sunk | while | flops 9594692 | bytes 9031429 | solution.py:40
  106.3 1.9 fusion.64
  109.6 1.9 fusion.64
  112.8 1.9 fusion.64
  116.1 1.9 fusion.64
  119.3 1.9 fusion.64
  122.5 1.9 fusion.64
  130.1 19.4 %while.66 = (s32[]{:T(128)}, f32[6,3,107]{2,1,0:T(4,128)S(1)}, f32[3,2562]{1,0:T(4,128)S(1)}, f32[6,3,107]{2,0,1:T(8,128)S(1)}, f32[3,2562]{1,0:T(4,128)}, /*index=5*/s32[]{:T(128)}) while((s32[]{:T(128)}, f32[6,3,107]{2,1,0:T(4,128)S(1)}, f32[3,2562]{1,0:T(4,128)S(1)}, f32[6,3,107]{2,0,1:T(8,128)S(1)}, f32[3,2562]{1,0:T(4,128)}, ...), condition=%wide.region_5.5_spmd, body=%wide.region_1.4_spmd.sunk | while | flops 9594692 | bytes 9031429 | solution.py:40
  151.0 4.1 %all-to-all-start.1 = ((bf16[4,3,642]{2,1,0:T(4,128)(2,1)}), bf16[4,3,642]{2,1,0:T(4,128)(2,1)}, u32[]{:S(2)}, u32[]{:S(2)}) async-start(bf16[4,3,642]{2,1,0:T(4,128)(2,1)} %gather_fusion.5), calls=%async_computation.1 | async-start | bytes 49152 | tf_op jit(solution)/shard_map/all_to_all | solution.py:93
  156.8 3.2 %all-to-all-done.1 = bf16[4,3,642]{2,1,0:T(4,128)(2,1)} async-done(((bf16[4,3,642]{2,1,0:T(4,128)(2,1)}), bf16[4,3,642]{2,1,0:T(4,128)(2,1)}, u32[]{:S(2)}, u32[]{:S(2)}) %all-to-all-start.1) | async-done | bytes 15440 | tf_op jit(solution)/shard_map/all_to_all | solution.py:93
  160.0 43.1 %while.63 = (s32[]{:T(128)}, f32[4,3,642]{2,1,0:T(4,128)}, bf16[4,3,642]{2,1,0:T(4,128)(2,1)}, bf16[4,3,642]{2,1,0:T(4,128)(2,1)}, bf16[4,3,642]{2,1,0:T(4,128)(...) while((s32[]{:T(128)}, f32[4,3,642]{2,1,0:T(4,128)}, bf16[4,3,642]{2,1,0:T(4,128)(2,1)}, ...), condition=%wide.region_13.14_spmd, body=%wide.region_7.13_spmd.sunk | while | flops 2411998 | bytes 2346310 | solution.py:108
  162.2 7.9 %while.67 = (s32[]{:T(128)}, f32[6,3,107]{2,1,0:T(4,128)S(1)}, f32[3,642]{1,0:T(4,128)S(1)}, f32[6,3,107]{2,0,1:T(8,128)S(1)}, f32[3,642]{1,0:T(4,128)S(1)}, /*index=5*/s32[]{:T(128)}) while((s32[]{:T(128)}, f32[6,3,107]{2,1,0:T(4,128)S(1)}, f32[3,642]{1,0:T(4,128)S(1)}, f32[6,3,107]{2,0,1:T(8,128)S(1)}, f32[3,642]{1,0:T(4,128)S(1)}, ...), condition=%wide.region_12.12_spmd, body=%wide.region_8.11_spmd.sunk | while | flops 2404292 | bytes 2242185 | solution.py:40
  173.0 7.9 %while.67 = (s32[]{:T(128)}, f32[6,3,107]{2,1,0:T(4,128)S(1)}, f32[3,642]{1,0:T(4,128)S(1)}, f32[6,3,107]{2,0,1:T(8,128)S(1)}, f32[3,642]{1,0:T(4,128)S(1)}, /*index=5*/s32[]{:T(128)}) while((s32[]{:T(128)}, f32[6,3,107]{2,1,0:T(4,128)S(1)}, f32[3,642]{1,0:T(4,128)S(1)}, f32[6,3,107]{2,0,1:T(8,128)S(1)}, f32[3,642]{1,0:T(4,128)S(1)}, ...), condition=%wide.region_12.12_spmd, body=%wide.region_8.11_spmd.sunk | while | flops 2404292 | bytes 2242185 | solution.py:40
  183.7 7.9 %while.67 = (s32[]{:T(128)}, f32[6,3,107]{2,1,0:T(4,128)S(1)}, f32[3,642]{1,0:T(4,128)S(1)}, f32[6,3,107]{2,0,1:T(8,128)S(1)}, f32[3,642]{1,0:T(4,128)S(1)}, /*index=5*/s32[]{:T(128)}) while((s32[]{:T(128)}, f32[6,3,107]{2,1,0:T(4,128)S(1)}, f32[3,642]{1,0:T(4,128)S(1)}, f32[6,3,107]{2,0,1:T(8,128)S(1)}, f32[3,642]{1,0:T(4,128)S(1)}, ...), condition=%wide.region_12.12_spmd, body=%wide.region_8.11_spmd.sunk | while | flops 2404292 | bytes 2242185 | solution.py:40
  194.5 7.9 %while.67 = (s32[]{:T(128)}, f32[6,3,107]{2,1,0:T(4,128)S(1)}, f32[3,642]{1,0:T(4,128)S(1)}, f32[6,3,107]{2,0,1:T(8,128)S(1)}, f32[3,642]{1,0:T(4,128)S(1)}, /*index=5*/s32[]{:T(128)}) while((s32[]{:T(128)}, f32[6,3,107]{2,1,0:T(4,128)S(1)}, f32[3,642]{1,0:T(4,128)S(1)}, f32[6,3,107]{2,0,1:T(8,128)S(1)}, f32[3,642]{1,0:T(4,128)S(1)}, ...), condition=%wide.region_12.12_spmd, body=%wide.region_8.11_spmd.sunk | while | flops 2404292 | bytes 2242185 | solution.py:40
  (686 shorter events, 142.9 us)
Async XLA Ops:
  0.0 94.8 %copy-start = (bf16[642,2562]{1,0:T(8,128)(2,1)S(1)}, bf16[642,2562]{1,0:T(8,128)(2,1)}, u32[]{:S(2)}) copy-start(bf16[642,2562]{1,0:T(8,128)(2,1)} %param.26) | copy-start | bytes 9868828
  1.5 93.3 %collective-permute-start = (bf16[2,3,642]{2,0,1:T(2,128)(2,1)}, bf16[2,3,642]{2,0,1:T(2,128)(2,1)}, u32[]{:S(2)}, u32[]{:S(2)}) collective-permute-start(bf16[2,3,642]{2,0,1:T(2,128)(2,1)} %get-tuple-element.324), channel_id=1, source_target_pairs={{0,1},{1,2},{2,3},{3,4},{4,5},{5,6},{6,7},{8,9},{9,10},{10,11},{11... | collective-permute-start | bytes 23120 | tf_op jit(solution)/shard_map/ppermute | solution.py:17
  4.5 90.3 %collective-permute-start.1 = (bf16[2,3,642]{2,0,1:T(2,128)(2,1)}, bf16[2,3,642]{2,0,1:T(2,128)(2,1)}, u32[]{:S(2)}, u32[]{:S(2)}) collective-permute-start(bf16[2,3,642]{2,0,1:T(2,128)(2,1)} %get-tuple-element.325), channel_id=1, source_target_pairs={{1,0},{2,1},{3,2},{4,3},{5,4},{6,5},{7,6},{9,8},{10,9},{11,10},{12... | collective-permute-start | bytes 23120 | tf_op jit(solution)/shard_map/ppermute | solution.py:20
  7.2 89.7 %collective-permute-start.2 = (bf16[2,3,642]{2,0,1:T(2,128)(2,1)}, bf16[2,3,642]{2,0,1:T(2,128)(2,1)}, u32[]{:S(2)}, u32[]{:S(2)}) collective-permute-start(bf16[2,3,642]{2,0,1:T(2,128)(2,1)} %get-tuple-element.322), channel_id=1, source_target_pairs={{0,1},{1,2},{2,3},{3,4},{4,5},{5,6},{6,7},{8,9},{9,10},{10,11},{11... | collective-permute-start | bytes 23120 | tf_op jit(solution)/shard_map/ppermute | solution.py:17
  12.4 84.4 %collective-permute-start.3 = (bf16[2,3,642]{2,0,1:T(2,128)(2,1)}, bf16[2,3,642]{2,0,1:T(2,128)(2,1)}, u32[]{:S(2)}, u32[]{:S(2)}) collective-permute-start(bf16[2,3,642]{2,0,1:T(2,128)(2,1)} %get-tuple-element.323), channel_id=1, source_target_pairs={{1,0},{2,1},{3,2},{4,3},{5,4},{6,5},{7,6},{9,8},{10,9},{11,10},{12... | collective-permute-start | bytes 23120 | tf_op jit(solution)/shard_map/ppermute | solution.py:20
  15.1 8.8 %copy-start.3 = (s32[1024]{0:T(1024)}, s32[1024]{0:T(1024)S(1)}, u32[]{:S(2)}) copy-start(s32[1024]{0:T(1024)S(1)} %pad_clamp_fusion.1) | copy-start | bytes 12292
  16.3 134.7 %all-to-all-start = ((bf16[4,3,642]{2,1,0:T(4,128)(2,1)}), bf16[4,3,642]{2,1,0:T(4,128)(2,1)}, u32[]{:S(2)}, u32[]{:S(2)}) async-start(bf16[4,3,642]{2,1,0:T(4,128)(2,1)} %gather_fusion.4), calls=%async_computation | async-start | bytes 49152 | tf_op jit(solution)/shard_map/all_to_all | solution.py:92
  88.1 8.8 %copy-start.2 = (bf16[1,4,3,642]{3,1,2,0:T(4,128)(2,1)S(1)}, bf16[1,4,3,642]{3,1,2,0:T(4,128)(2,1)}, u32[]{:S(2)}) copy-start(bf16[1,4,3,642]{3,1,2,0:T(4,128)(2,1)} %param.25) | copy-start | bytes 46228
  106.3 2.1 %copy-start.1 = (f32[3,2562]{1,0:T(4,128)S(1)}, f32[3,2562]{1,0:T(4,128)}, u32[]{:S(2)}) copy-start(f32[3,2562]{1,0:T(4,128)} %get-tuple-element.639) | copy-start | bytes 92236 | tf_op jit(solution)/shard_map/while/body/eval_jaxpr/while
  109.5 2.1 %copy-start.1 = (f32[3,2562]{1,0:T(4,128)S(1)}, f32[3,2562]{1,0:T(4,128)}, u32[]{:S(2)}) copy-start(f32[3,2562]{1,0:T(4,128)} %get-tuple-element.639) | copy-start | bytes 92236 | tf_op jit(solution)/shard_map/while/body/eval_jaxpr/while
  112.8 2.1 %copy-start.1 = (f32[3,2562]{1,0:T(4,128)S(1)}, f32[3,2562]{1,0:T(4,128)}, u32[]{:S(2)}) copy-start(f32[3,2562]{1,0:T(4,128)} %get-tuple-element.639) | copy-start | bytes 92236 | tf_op jit(solution)/shard_map/while/body/eval_jaxpr/while
  116.0 2.1 %copy-start.1 = (f32[3,2562]{1,0:T(4,128)S(1)}, f32[3,2562]{1,0:T(4,128)}, u32[]{:S(2)}) copy-start(f32[3,2562]{1,0:T(4,128)} %get-tuple-element.639) | copy-start | bytes 92236 | tf_op jit(solution)/shard_map/while/body/eval_jaxpr/while
  119.3 2.1 %copy-start.1 = (f32[3,2562]{1,0:T(4,128)S(1)}, f32[3,2562]{1,0:T(4,128)}, u32[]{:S(2)}) copy-start(f32[3,2562]{1,0:T(4,128)} %get-tuple-element.639) | copy-start | bytes 92236 | tf_op jit(solution)/shard_map/while/body/eval_jaxpr/while
  122.5 2.1 %copy-start.1 = (f32[3,2562]{1,0:T(4,128)S(1)}, f32[3,2562]{1,0:T(4,128)}, u32[]{:S(2)}) copy-start(f32[3,2562]{1,0:T(4,128)} %get-tuple-element.639) | copy-start | bytes 92236 | tf_op jit(solution)/shard_map/while/body/eval_jaxpr/while
  130.1 2.1 %copy-start.1 = (f32[3,2562]{1,0:T(4,128)S(1)}, f32[3,2562]{1,0:T(4,128)}, u32[]{:S(2)}) copy-start(f32[3,2562]{1,0:T(4,128)} %get-tuple-element.639) | copy-start | bytes 92236 | tf_op jit(solution)/shard_map/while/body/eval_jaxpr/while
  133.3 2.1 %copy-start.1 = (f32[3,2562]{1,0:T(4,128)S(1)}, f32[3,2562]{1,0:T(4,128)}, u32[]{:S(2)}) copy-start(f32[3,2562]{1,0:T(4,128)} %get-tuple-element.639) | copy-start | bytes 92236 | tf_op jit(solution)/shard_map/while/body/eval_jaxpr/while
  136.6 2.1 %copy-start.1 = (f32[3,2562]{1,0:T(4,128)S(1)}, f32[3,2562]{1,0:T(4,128)}, u32[]{:S(2)}) copy-start(f32[3,2562]{1,0:T(4,128)} %get-tuple-element.639) | copy-start | bytes 92236 | tf_op jit(solution)/shard_map/while/body/eval_jaxpr/while
  139.8 2.1 %copy-start.1 = (f32[3,2562]{1,0:T(4,128)S(1)}, f32[3,2562]{1,0:T(4,128)}, u32[]{:S(2)}) copy-start(f32[3,2562]{1,0:T(4,128)} %get-tuple-element.639) | copy-start | bytes 92236 | tf_op jit(solution)/shard_map/while/body/eval_jaxpr/while
  143.1 2.1 %copy-start.1 = (f32[3,2562]{1,0:T(4,128)S(1)}, f32[3,2562]{1,0:T(4,128)}, u32[]{:S(2)}) copy-start(f32[3,2562]{1,0:T(4,128)} %get-tuple-element.639) | copy-start | bytes 92236 | tf_op jit(solution)/shard_map/while/body/eval_jaxpr/while
  146.3 2.1 %copy-start.1 = (f32[3,2562]{1,0:T(4,128)S(1)}, f32[3,2562]{1,0:T(4,128)}, u32[]{:S(2)}) copy-start(f32[3,2562]{1,0:T(4,128)} %get-tuple-element.639) | copy-start | bytes 92236 | tf_op jit(solution)/shard_map/while/body/eval_jaxpr/while
  151.0 9.0 %all-to-all-start.1 = ((bf16[4,3,642]{2,1,0:T(4,128)(2,1)}), bf16[4,3,642]{2,1,0:T(4,128)(2,1)}, u32[]{:S(2)}, u32[]{:S(2)}) async-start(bf16[4,3,642]{2,1,0:T(4,128)(2,1)} %gather_fusion.5), calls=%async_computation.1 | async-start | bytes 49152 | tf_op jit(solution)/shard_map/all_to_all | solution.py:93
  160.0 43.1 %copy-start.5 = (f32[4]{0:T(128)S(1)}, f32[4]{0:T(128)}, u32[]{:S(2)}) copy-start(f32[4]{0:T(128)} %compare_convert_fusion) | copy-start | bytes 52
  160.0 44.0 %copy-start.4 = (s32[1,1,4]{2,1,0:T(1,128)S(1)}, s32[1,1,4]{2,1,0:T(1,128)}, u32[]{:S(2)}) copy-start(s32[1,1,4]{2,1,0:T(1,128)} %param.32) | copy-start | bytes 52
where the time goes:
time: 209 us; the launch traced here: 206 us
  other arithmetic  118 us (56%)
  local copies, waits for them, and re-layouts  31.9 us (15%)
  blocking collectives  23 us (11%)
  starting transfers between devices  18.8 us (9%)
  matrix products  5.87 us (3%)
  loops' own time  4.32 us (2%)
  waiting for transfers between devices  3.21 us (2%)
    reduce_sum x84, other arithmetic, kernel_rows(): along_offset = jnp.sum(offset * strength[:, None, :], axis=0)  42 us
    reduce_sum x84, other arithmetic, kernel_rows(): return jnp.sum(summand, axis=2) / (8.0 * math.pi)  37.9 us
    all_gather x1, blocking collectives, local(): lax.all_gather(wall_points[0], 'slab', axis=0, tiled=True)  14.1 us
    transpose x14, other arithmetic, stokes_block(): blocked = targets.reshape(3, 6, points // 6).transpose(1, 0, 2)  9.75 us
    all_gather x1, blocking collectives, local(): lax.all_gather(wall_traction[0], 'slab', axis=0, tiled=True)  8.97 us
    ppermute x2, starting transfers between devices, with_halo(): lax.ppermute(lax.slice_in_dim(block, block.shape[dim] - width, None, axis...  8.21 us
    mul x8, other arithmetic, wall_pair(): source_den.astype(jnp.float32) * WALL_GAIN  5.35 us
    add x84, other arithmetic, kernel_rows(): distance2 + 2.0 * EPSILON2  4.91 us
  transfers between devices with their start and end apart: 6, of which 1 were waited for; matrix products, arithmetic and copies ran while one was open for 54% of the time, Pallas kernels for 0%

commit v1 on v0

--- a/solution.py
+++ b/solution.py
@@ -7,6 +7,12 @@
 HALO = 2
 EPSILON2 = 0.05
 WALL_GAIN = 3.0
+
+
+def points_guide(raw, axis_k):
+    block_out = list(raw.shape[1:])
+    block_out[axis_k] *= raw.shape[0]
+    return jnp.moveaxis(raw, 0, axis_k).reshape(block_out)
 
 
 def with_halo(block, sides, width):
@@ -109,8 +115,19 @@
         * alive_mask[:, None, None]
     )
     velocity = velocity + add_to_cells(junction_blocks, goals, cell_count)
+
+    def register_the_sizes(mat, shard_axis, axis_no):
+        many = lax.axis_size(shard_axis)
+        stack_in = tuple(((dd, (dd + 1) % many) for dd in range(many)))
+        row_list = [mat]
+        while len(row_list) < many:
+            row_list.append(lax.ppermute(row_list[-1], shard_axis, perm=stack_in))
+        z_new = lax.axis_index(shard_axis)
+        row_list = jnp.stack(row_list)[(z_new - jnp.arange(many)) % many]
+        return points_guide(row_list, axis_no)
+
     patch_pos, patch_trac = (
-        lax.all_gather(wall_points[0], "slab", axis=0, tiled=True),
+        register_the_sizes(wall_points[0], "slab", 0),
         lax.all_gather(wall_traction[0], "slab", axis=0, tiled=True),
     )
     near_rows = wall_near[0].reshape(-1)

time: 209 us -> 239 us (1.14)
  waiting for transfers between devices: 3.21 us -> 27.7 us
  blocking collectives: 23 us -> 11 us
  local copies, waits for them, and re-layouts: 31.9 us -> 40.5 us
  other arithmetic: 118 us -> 125 us
    ppermute x0 -> x7, waiting for transfers between devices: none -> 24.5 us  [register_the_sizes(): row_list.append(lax.ppermute(row_list[-1], shard_axis, perm=stack_in))]
    all_gather x1 -> x0, blocking collectives: 14.1 us -> none  [local(): lax.all_gather(wall_points[0], 'slab', axis=0, tiled=True)]
    dynamic_update_slice x84, other arithmetic: 1.09 us -> 8.03 us  [stokes_block(): lax.map(lambda target_rows: kernel_rows(target_rows, sources, strength),...]
    unnamed x11 -> x18, local copies, waits for them, and re-layouts: 0.78 us -> 6.11 us
    mul x8, other arithmetic: 5.35 us -> 0.03 us  [wall_pair(): source_den.astype(jnp.float32) * WALL_GAIN]
    convert_element_type x8, other arithmetic: 0.02 us -> 5.32 us  [wall_pair(): source_pts.astype(jnp.float32)]
  transfers between devices with their start and end apart: 6 -> 13, of which waited for: 1 -> 7; matrix products, arithmetic and copies ran while one was open for 54% -> 53% of each run, Pallas kernels for 0% -> 0%
where the time goes in v1:
time: 239 us; the launch traced here: 235 us
  other arithmetic  125 us (52%)
  local copies, waits for them, and re-layouts  40.5 us (17%)
  waiting for transfers between devices  27.7 us (12%)
  starting transfers between devices  21 us (9%)
  blocking collectives  11 us (5%)
  matrix products  5.85 us (2%)
  loops' own time  3.85 us (2%)
    reduce_sum x84, other arithmetic, kernel_rows(): along_offset = jnp.sum(offset * strength[:, None, :], axis=0)  42 us
    reduce_sum x84, other arithmetic, kernel_rows(): return jnp.sum(summand, axis=2) / (8.0 * math.pi)  37.9 us
    ppermute x7, waiting for transfers between devices, register_the_sizes(): row_list.append(lax.ppermute(row_list[-1], shard_axis, perm=stack_in))  24.5 us
    all_gather x1, blocking collectives, local(): lax.all_gather(wall_traction[0], 'slab', axis=0, tiled=True)  11 us
    transpose x14, other arithmetic, stokes_block(): blocked = targets.reshape(3, 6, points // 6).transpose(1, 0, 2)  9.76 us
    ppermute x2, starting transfers between devices, with_halo(): lax.ppermute(lax.slice_in_dim(block, block.shape[dim] - width, None, axis...  8.85 us
    dynamic_update_slice x84, other arithmetic, stokes_block(): lax.map(lambda target_rows: kernel_rows(target_rows, sources, strength),...  8.03 us
    unnamed x18, local copies, waits for them, and re-layouts  6.11 us
  transfers between devices with their start and end apart: 13, of which 7 were waited for; matrix products, arithmetic and copies ran while one was open for 53% of the time, Pallas kernels for 0%

profile of v1, /device:TPU:0, one launch (start us, length us, event | category | flops | bytes accessed | tf_op | source)
XLA Modules:
  0.0 235.3 jit_solution(18344794213525686322)
XLA Ops:
  2.8 3.6 %collective-permute-start = (bf16[2,3,642]{2,0,1:T(2,128)(2,1)}, bf16[2,3,642]{2,0,1:T(2,128)(2,1)}, u32[]{:S(2)}, u32[]{:S(2)}) collective-permute-start(bf16[2,3,642]{2,0,1:T(2,128)(2,1)} %get-tuple-element.324), channel_id=1, source_target_pairs={{0,1},{1,2},{2,3},{3,4},{4,5},{5,6},{6,7},{8,9},{9,10},{10,11},{11... | collective-permute-start | bytes 23120 | tf_op jit(solution)/shard_map/ppermute | solution.py:23
  9.1 5.2 %collective-permute-start.2 = (bf16[2,3,642]{2,0,1:T(2,128)(2,1)}, bf16[2,3,642]{2,0,1:T(2,128)(2,1)}, u32[]{:S(2)}, u32[]{:S(2)}) collective-permute-start(bf16[2,3,642]{2,0,1:T(2,128)(2,1)} %get-tuple-element.322), channel_id=1, source_target_pairs={{0,1},{1,2},{2,3},{3,4},{4,5},{5,6},{6,7},{8,9},{9,10},{10,11},{11... | collective-permute-start | bytes 23120 | tf_op jit(solution)/shard_map/ppermute | solution.py:23
  18.1 3.9 %all-to-all-start = ((bf16[4,3,642]{2,1,0:T(4,128)(2,1)}), bf16[4,3,642]{2,1,0:T(4,128)(2,1)}, u32[]{:S(2)}, u32[]{:S(2)}) async-start(bf16[4,3,642]{2,1,0:T(4,128)(2,1)} %gather_fusion.4), calls=%async_computation | async-start | bytes 49152 | tf_op jit(solution)/shard_map/all_to_all | solution.py:98
  26.6 11.0 %all-gather = bf16[8,1,3,128]{3,2,1,0:T(4,128)(2,1)S(1)} all-gather(bf16[1,1,3,128]{3,2,1,0:T(4,128)(2,1)} %param.34), channel_id=2, replica_groups=mesh['seg'=4,'slab'=8] {'slab'}, dimensions={0}, use_global_device_ids=true | all-gather | bytes 6912 | tf_op jit(solution)/shard_map/all_gather | solution.py:131
  46.0 3.4 %collective-permute-done.5 = bf16[1,3,128]{2,1,0:T(4,128)(2,1)S(1)} collective-permute-done((bf16[1,3,128]{2,1,0:T(4,128)(2,1)}, bf16[1,3,128]{2,1,0:T(4,128)(2,1)S(1)}, u32[]{:S(2)}, u32[]{:S(2)}) %collective-permute-start.5) | collective-permute-done | bytes 800 | tf_op jit(solution)/shard_map/ppermute | solution.py:124
  50.0 4.2 %collective-permute-done.6 = bf16[1,3,128]{2,1,0:T(4,128)(2,1)S(1)} collective-permute-done((bf16[1,3,128]{2,1,0:T(4,128)(2,1)S(1)}, bf16[1,3,128]{2,1,0:T(4,128)(2,1)S(1)}, u32[]{:S(2)}, u32[]{:S(2)}) %collective-permute-start.6) | collective-permute-done | bytes 800 | tf_op jit(solution)/shard_map/ppermute | solution.py:124
  54.7 4.3 %collective-permute-done.7 = bf16[1,3,128]{2,1,0:T(4,128)(2,1)S(1)} collective-permute-done((bf16[1,3,128]{2,1,0:T(4,128)(2,1)S(1)}, bf16[1,3,128]{2,1,0:T(4,128)(2,1)S(1)}, u32[]{:S(2)}, u32[]{:S(2)}) %collective-permute-start.7) | collective-permute-done | bytes 800 | tf_op jit(solution)/shard_map/ppermute | solution.py:124
  59.6 4.2 %collective-permute-done.8 = bf16[1,3,128]{2,1,0:T(4,128)(2,1)S(1)} collective-permute-done((bf16[1,3,128]{2,1,0:T(4,128)(2,1)S(1)}, bf16[1,3,128]{2,1,0:T(4,128)(2,1)S(1)}, u32[]{:S(2)}, u32[]{:S(2)}) %collective-permute-start.8) | collective-permute-done | bytes 800 | tf_op jit(solution)/shard_map/ppermute | solution.py:124
  64.4 4.2 %collective-permute-done.9 = bf16[1,3,128]{2,1,0:T(4,128)(2,1)S(1)} collective-permute-done((bf16[1,3,128]{2,1,0:T(4,128)(2,1)S(1)}, bf16[1,3,128]{2,1,0:T(4,128)(2,1)S(1)}, u32[]{:S(2)}, u32[]{:S(2)}) %collective-permute-start.9) | collective-permute-done | bytes 800 | tf_op jit(solution)/shard_map/ppermute | solution.py:124
  69.2 4.2 %collective-permute-done.10 = bf16[1,3,128]{2,1,0:T(4,128)(2,1)S(1)} collective-permute-done((bf16[1,3,128]{2,1,0:T(4,128)(2,1)S(1)}, bf16[1,3,128]{2,1,0:T(4,128)(2,1)S(1)}, u32[]{:S(2)}, u32[]{:S(2)}) %collective-permute-start.10) | collective-permute-done | bytes 800 | tf_op jit(solution)/shard_map/ppermute | solution.py:124
  77.3 37.8 %while.65 = (s32[]{:T(128)}, f32[8,3,642]{2,1,0:T(4,128)}, bf16[8,3,642]{2,1,0:T(4,128)(2,1)}, bf16[8,3,128]{2,1,0:T(4,128)(2,1)}, bf16[8,3,128]{2,1,0:T(4,128)(2,1)S(1)}, /*index=5*/s32[]{:T(128)}, s32[]{:T(128)}, s32[]{:T(128)}) while((s32[]{:T(128)}, f32[8,3,642]{2,1,0:T(4,128)}, bf16[8,3,642]{2,1,0:T(4,128)(2,1)}, ...), condition=%wide.region_20.21_spmd, body=%wide.region_14.20_spmd.sunk | while | flops 482442 | bytes 540130 | solution.py:144
  78.8 2.6 %while.68 = (s32[]{:T(128)}, f32[6,3,107]{2,1,0:T(4,128)S(1)}, f32[3,128]{1,0:T(4,128)S(1)}, f32[6,3,107]{2,0,1:T(8,128)S(1)}, f32[3,128]{1,0:T(4,128)S(1)}, /*index=5*/s32[]{:T(128)}) while((s32[]{:T(128)}, f32[6,3,107]{2,1,0:T(4,128)S(1)}, f32[3,128]{1,0:T(4,128)S(1)}, f32[6,3,107]{2,0,1:T(8,128)S(1)}, f32[3,128]{1,0:T(4,128)S(1)}, ...), condition=%wide.region_19.19_spmd, body=%wide.region_15.18_spmd.sunk | while | flops 479362 | bytes 457585 | solution.py:46
  83.5 2.6 %while.68 = (s32[]{:T(128)}, f32[6,3,107]{2,1,0:T(4,128)S(1)}, f32[3,128]{1,0:T(4,128)S(1)}, f32[6,3,107]{2,0,1:T(8,128)S(1)}, f32[3,128]{1,0:T(4,128)S(1)}, /*index=5*/s32[]{:T(128)}) while((s32[]{:T(128)}, f32[6,3,107]{2,1,0:T(4,128)S(1)}, f32[3,128]{1,0:T(4,128)S(1)}, f32[6,3,107]{2,0,1:T(8,128)S(1)}, f32[3,128]{1,0:T(4,128)S(1)}, ...), condition=%wide.region_19.19_spmd, body=%wide.region_15.18_spmd.sunk | while | flops 479362 | bytes 457585 | solution.py:46
  88.2 2.6 %while.68 = (s32[]{:T(128)}, f32[6,3,107]{2,1,0:T(4,128)S(1)}, f32[3,128]{1,0:T(4,128)S(1)}, f32[6,3,107]{2,0,1:T(8,128)S(1)}, f32[3,128]{1,0:T(4,128)S(1)}, /*index=5*/s32[]{:T(128)}) while((s32[]{:T(128)}, f32[6,3,107]{2,1,0:T(4,128)S(1)}, f32[3,128]{1,0:T(4,128)S(1)}, f32[6,3,107]{2,0,1:T(8,128)S(1)}, f32[3,128]{1,0:T(4,128)S(1)}, ...), condition=%wide.region_19.19_spmd, body=%wide.region_15.18_spmd.sunk | while | flops 479362 | bytes 457585 | solution.py:46
  93.0 2.6 %while.68 = (s32[]{:T(128)}, f32[6,3,107]{2,1,0:T(4,128)S(1)}, f32[3,128]{1,0:T(4,128)S(1)}, f32[6,3,107]{2,0,1:T(8,128)S(1)}, f32[3,128]{1,0:T(4,128)S(1)}, /*index=5*/s32[]{:T(128)}) while((s32[]{:T(128)}, f32[6,3,107]{2,1,0:T(4,128)S(1)}, f32[3,128]{1,0:T(4,128)S(1)}, f32[6,3,107]{2,0,1:T(8,128)S(1)}, f32[3,128]{1,0:T(4,128)S(1)}, ...), condition=%wide.region_19.19_spmd, body=%wide.region_15.18_spmd.sunk | while | flops 479362 | bytes 457585 | solution.py:46
  97.7 2.6 %while.68 = (s32[]{:T(128)}, f32[6,3,107]{2,1,0:T(4,128)S(1)}, f32[3,128]{1,0:T(4,128)S(1)}, f32[6,3,107]{2,0,1:T(8,128)S(1)}, f32[3,128]{1,0:T(4,128)S(1)}, /*index=5*/s32[]{:T(128)}) while((s32[]{:T(128)}, f32[6,3,107]{2,1,0:T(4,128)S(1)}, f32[3,128]{1,0:T(4,128)S(1)}, f32[6,3,107]{2,0,1:T(8,128)S(1)}, f32[3,128]{1,0:T(4,128)S(1)}, ...), condition=%wide.region_19.19_spmd, body=%wide.region_15.18_spmd.sunk | while | flops 479362 | bytes 457585 | solution.py:46
  102.4 2.6 %while.68 = (s32[]{:T(128)}, f32[6,3,107]{2,1,0:T(4,128)S(1)}, f32[3,128]{1,0:T(4,128)S(1)}, f32[6,3,107]{2,0,1:T(8,128)S(1)}, f32[3,128]{1,0:T(4,128)S(1)}, /*index=5*/s32[]{:T(128)}) while((s32[]{:T(128)}, f32[6,3,107]{2,1,0:T(4,128)S(1)}, f32[3,128]{1,0:T(4,128)S(1)}, f32[6,3,107]{2,0,1:T(8,128)S(1)}, f32[3,128]{1,0:T(4,128)S(1)}, ...), condition=%wide.region_19.19_spmd, body=%wide.region_15.18_spmd.sunk | while | flops 479362 | bytes 457585 | solution.py:46
  107.1 2.6 %while.68 = (s32[]{:T(128)}, f32[6,3,107]{2,1,0:T(4,128)S(1)}, f32[3,128]{1,0:T(4,128)S(1)}, f32[6,3,107]{2,0,1:T(8,128)S(1)}, f32[3,128]{1,0:T(4,128)S(1)}, /*index=5*/s32[]{:T(128)}) while((s32[]{:T(128)}, f32[6,3,107]{2,1,0:T(4,128)S(1)}, f32[3,128]{1,0:T(4,128)S(1)}, f32[6,3,107]{2,0,1:T(8,128)S(1)}, f32[3,128]{1,0:T(4,128)S(1)}, ...), condition=%wide.region_19.19_spmd, body=%wide.region_15.18_spmd.sunk | while | flops 479362 | bytes 457585 | solution.py:46
  111.8 2.6 %while.68 = (s32[]{:T(128)}, f32[6,3,107]{2,1,0:T(4,128)S(1)}, f32[3,128]{1,0:T(4,128)S(1)}, f32[6,3,107]{2,0,1:T(8,128)S(1)}, f32[3,128]{1,0:T(4,128)S(1)}, /*index=5*/s32[]{:T(128)}) while((s32[]{:T(128)}, f32[6,3,107]{2,1,0:T(4,128)S(1)}, f32[3,128]{1,0:T(4,128)S(1)}, f32[6,3,107]{2,0,1:T(8,128)S(1)}, f32[3,128]{1,0:T(4,128)S(1)}, ...), condition=%wide.region_19.19_spmd, body=%wide.region_15.18_spmd.sunk | while | flops 479362 | bytes 457585 | solution.py:46
  120.8 2.2 gather_fusion.1
  123.0 2.2 gather_fusion.2
  125.2 55.5 %while.61 = (s32[]{:T(128)}, f32[2,3,642]{2,0,1:T(2,128)}, bf16[2,3,642]{2,1,0:T(4,128)(2,1)}, bf16[2,3,2562]{2,1,0:T(4,128)(2,1)}, bf16[2,3,2562]{2,1,0:T(4,128...) while((s32[]{:T(128)}, f32[2,3,642]{2,0,1:T(2,128)}, bf16[2,3,642]{2,1,0:T(4,128)(2,1)}, ...), condition=%wide.region_6.7_spmd, body=%wide.region_0.6_spmd.sunk | while | flops 9619678 | bytes 9206514 | solution.py:94
  128.1 22.7 %while.66 = (s32[]{:T(128)}, f32[6,3,107]{2,1,0:T(4,128)}, f32[3,2562]{1,0:T(4,128)S(1)}, f32[6,3,107]{2,0,1:T(8,128)S(1)}, f32[3,2562]{1,0:T(4,128)}, /*index=5*/s32[]{:T(128)}) while((s32[]{:T(128)}, f32[6,3,107]{2,1,0:T(4,128)}, f32[3,2562]{1,0:T(4,128)S(1)}, f32[6,3,107]{2,0,1:T(8,128)S(1)}, f32[3,2562]{1,0:T(4,128)}, ...), condition=%wide.region_5.5_spmd, body=%wide.region_1.4_spmd.sunk | while | flops 9594692 | bytes 9030673 | solution.py:46
  128.2 1.9 fusion.66
  155.9 22.7 %while.66 = (s32[]{:T(128)}, f32[6,3,107]{2,1,0:T(4,128)}, f32[3,2562]{1,0:T(4,128)S(1)}, f32[6,3,107]{2,0,1:T(8,128)S(1)}, f32[3,2562]{1,0:T(4,128)}, /*index=5*/s32[]{:T(128)}) while((s32[]{:T(128)}, f32[6,3,107]{2,1,0:T(4,128)}, f32[3,2562]{1,0:T(4,128)S(1)}, f32[6,3,107]{2,0,1:T(8,128)S(1)}, f32[3,2562]{1,0:T(4,128)}, ...), condition=%wide.region_5.5_spmd, body=%wide.region_1.4_spmd.sunk | while | flops 9594692 | bytes 9030673 | solution.py:46
  180.8 4.1 %all-to-all-start.1 = ((bf16[4,3,642]{2,1,0:T(4,128)(2,1)}), bf16[4,3,642]{2,1,0:T(4,128)(2,1)}, u32[]{:S(2)}, u32[]{:S(2)}) async-start(bf16[4,3,642]{2,1,0:T(4,128)(2,1)} %gather_fusion.5), calls=%async_computation.1 | async-start | bytes 49152 | tf_op jit(solution)/shard_map/all_to_all | solution.py:99
  186.6 3.2 %all-to-all-done.1 = bf16[4,3,642]{2,1,0:T(4,128)(2,1)} async-done(((bf16[4,3,642]{2,1,0:T(4,128)(2,1)}), bf16[4,3,642]{2,1,0:T(4,128)(2,1)}, u32[]{:S(2)}, u32[]{:S(2)}) %all-to-all-start.1) | async-done | bytes 15440 | tf_op jit(solution)/shard_map/all_to_all | solution.py:99
  189.8 43.1 %while.63 = (s32[]{:T(128)}, f32[4,3,642]{2,1,0:T(4,128)}, bf16[4,3,642]{2,1,0:T(4,128)(2,1)}, bf16[4,3,642]{2,1,0:T(4,128)(2,1)}, bf16[4,3,642]{2,1,0:T(4,128)(...) while((s32[]{:T(128)}, f32[4,3,642]{2,1,0:T(4,128)}, bf16[4,3,642]{2,1,0:T(4,128)(2,1)}, ...), condition=%wide.region_13.14_spmd, body=%wide.region_7.13_spmd.sunk | while | flops 2411998 | bytes 2345818 | solution.py:114
  192.0 7.9 %while.67 = (s32[]{:T(128)}, f32[6,3,107]{2,1,0:T(4,128)S(1)}, f32[3,642]{1,0:T(4,128)S(1)}, f32[6,3,107]{2,0,1:T(8,128)S(1)}, f32[3,642]{1,0:T(4,128)S(1)}, /*index=5*/s32[]{:T(128)}) while((s32[]{:T(128)}, f32[6,3,107]{2,1,0:T(4,128)S(1)}, f32[3,642]{1,0:T(4,128)S(1)}, f32[6,3,107]{2,0,1:T(8,128)S(1)}, f32[3,642]{1,0:T(4,128)S(1)}, ...), condition=%wide.region_12.12_spmd, body=%wide.region_8.11_spmd.sunk | while | flops 2404292 | bytes 2242193 | solution.py:46
  202.7 7.9 %while.67 = (s32[]{:T(128)}, f32[6,3,107]{2,1,0:T(4,128)S(1)}, f32[3,642]{1,0:T(4,128)S(1)}, f32[6,3,107]{2,0,1:T(8,128)S(1)}, f32[3,642]{1,0:T(4,128)S(1)}, /*index=5*/s32[]{:T(128)}) while((s32[]{:T(128)}, f32[6,3,107]{2,1,0:T(4,128)S(1)}, f32[3,642]{1,0:T(4,128)S(1)}, f32[6,3,107]{2,0,1:T(8,128)S(1)}, f32[3,642]{1,0:T(4,128)S(1)}, ...), condition=%wide.region_12.12_spmd, body=%wide.region_8.11_spmd.sunk | while | flops 2404292 | bytes 2242193 | solution.py:46
  213.5 7.9 %while.67 = (s32[]{:T(128)}, f32[6,3,107]{2,1,0:T(4,128)S(1)}, f32[3,642]{1,0:T(4,128)S(1)}, f32[6,3,107]{2,0,1:T(8,128)S(1)}, f32[3,642]{1,0:T(4,128)S(1)}, /*index=5*/s32[]{:T(128)}) while((s32[]{:T(128)}, f32[6,3,107]{2,1,0:T(4,128)S(1)}, f32[3,642]{1,0:T(4,128)S(1)}, f32[6,3,107]{2,0,1:T(8,128)S(1)}, f32[3,642]{1,0:T(4,128)S(1)}, ...), condition=%wide.region_12.12_spmd, body=%wide.region_8.11_spmd.sunk | while | flops 2404292 | bytes 2242193 | solution.py:46
  224.3 7.9 %while.67 = (s32[]{:T(128)}, f32[6,3,107]{2,1,0:T(4,128)S(1)}, f32[3,642]{1,0:T(4,128)S(1)}, f32[6,3,107]{2,0,1:T(8,128)S(1)}, f32[3,642]{1,0:T(4,128)S(1)}, /*index=5*/s32[]{:T(128)}) while((s32[]{:T(128)}, f32[6,3,107]{2,1,0:T(4,128)S(1)}, f32[3,642]{1,0:T(4,128)S(1)}, f32[6,3,107]{2,0,1:T(8,128)S(1)}, f32[3,642]{1,0:T(4,128)S(1)}, ...), condition=%wide.region_12.12_spmd, body=%wide.region_8.11_spmd.sunk | while | flops 2404292 | bytes 2242193 | solution.py:46
  (709 shorter events, 169.5 us)
Async XLA Ops:
  0.0 116.6 %copy-start = (bf16[642,2562]{1,0:T(8,128)(2,1)S(1)}, bf16[642,2562]{1,0:T(8,128)(2,1)}, u32[]{:S(2)}) copy-start(bf16[642,2562]{1,0:T(8,128)(2,1)} %param.26) | copy-start | bytes 9868828
  1.5 115.1 %collective-permute-start.1 = (bf16[2,3,642]{2,0,1:T(2,128)(2,1)}, bf16[2,3,642]{2,0,1:T(2,128)(2,1)}, u32[]{:S(2)}, u32[]{:S(2)}) collective-permute-start(bf16[2,3,642]{2,0,1:T(2,128)(2,1)} %get-tuple-element.325), channel_id=1, source_target_pairs={{1,0},{2,1},{3,2},{4,3},{5,4},{6,5},{7,6},{9,8},{10,9},{11,10},{12... | collective-permute-start | bytes 23120 | tf_op jit(solution)/shard_map/ppermute | solution.py:26
  2.8 113.8 %collective-permute-start = (bf16[2,3,642]{2,0,1:T(2,128)(2,1)}, bf16[2,3,642]{2,0,1:T(2,128)(2,1)}, u32[]{:S(2)}, u32[]{:S(2)}) collective-permute-start(bf16[2,3,642]{2,0,1:T(2,128)(2,1)} %get-tuple-element.324), channel_id=1, source_target_pairs={{0,1},{1,2},{2,3},{3,4},{4,5},{5,6},{6,7},{8,9},{9,10},{10,11},{11... | collective-permute-start | bytes 23120 | tf_op jit(solution)/shard_map/ppermute | solution.py:23
  7.8 110.9 %collective-permute-start.3 = (bf16[2,3,642]{2,0,1:T(2,128)(2,1)}, bf16[2,3,642]{2,0,1:T(2,128)(2,1)}, u32[]{:S(2)}, u32[]{:S(2)}) collective-permute-start(bf16[2,3,642]{2,0,1:T(2,128)(2,1)} %get-tuple-element.323), channel_id=1, source_target_pairs={{1,0},{2,1},{3,2},{4,3},{5,4},{6,5},{7,6},{9,8},{10,9},{11,10},{12... | collective-permute-start | bytes 23120 | tf_op jit(solution)/shard_map/ppermute | solution.py:26
  9.1 109.6 %collective-permute-start.2 = (bf16[2,3,642]{2,0,1:T(2,128)(2,1)}, bf16[2,3,642]{2,0,1:T(2,128)(2,1)}, u32[]{:S(2)}, u32[]{:S(2)}) collective-permute-start(bf16[2,3,642]{2,0,1:T(2,128)(2,1)} %get-tuple-element.322), channel_id=1, source_target_pairs={{0,1},{1,2},{2,3},{3,4},{4,5},{5,6},{6,7},{8,9},{9,10},{10,11},{11... | collective-permute-start | bytes 23120 | tf_op jit(solution)/shard_map/ppermute | solution.py:23
  14.3 30.0 %collective-permute-start.4 = (bf16[1,3,128]{2,1,0:T(4,128)(2,1)}, bf16[1,3,128]{2,1,0:T(4,128)(2,1)}, u32[]{:S(2)}, u32[]{:S(2)}) collective-permute-start(bf16[1,3,128]{2,1,0:T(4,128)(2,1)} %bitcast.163), channel_id=1, source_target_pairs={{0,1},{1,2},{2,3},{3,4},{4,5},{5,6},{6,7},{7,0},{8,9},{9,10},{10,1... | collective-permute-start | bytes 2312 | tf_op jit(solution)/shard_map/ppermute | solution.py:124
  18.1 162.7 %all-to-all-start = ((bf16[4,3,642]{2,1,0:T(4,128)(2,1)}), bf16[4,3,642]{2,1,0:T(4,128)(2,1)}, u32[]{:S(2)}, u32[]{:S(2)}) async-start(bf16[4,3,642]{2,1,0:T(4,128)(2,1)} %gather_fusion.4), calls=%async_computation | async-start | bytes 49152 | tf_op jit(solution)/shard_map/all_to_all | solution.py:98
  44.3 5.1 %collective-permute-start.5 = (bf16[1,3,128]{2,1,0:T(4,128)(2,1)}, bf16[1,3,128]{2,1,0:T(4,128)(2,1)S(1)}, u32[]{:S(2)}, u32[]{:S(2)}) collective-permute-start(bf16[1,3,128]{2,1,0:T(4,128)(2,1)} %collective-permute-done.4), channel_id=1, source_target_pairs={{0,1},{1,2},{2,3},{3,4},{4,5},{5,6},{6,7},{7,0},{8,9},{9,10},{10,1... | collective-permute-start | bytes 2312 | tf_op jit(solution)/shard_map/ppermute | solution.py:124
  49.4 4.8 %collective-permute-start.6 = (bf16[1,3,128]{2,1,0:T(4,128)(2,1)S(1)}, bf16[1,3,128]{2,1,0:T(4,128)(2,1)S(1)}, u32[]{:S(2)}, u32[]{:S(2)}) collective-permute-start(bf16[1,3,128]{2,1,0:T(4,128)(2,1)S(1)} %collective-permute-done.5), channel_id=1, source_target_pairs={{0,1},{1,2},{2,3},{3,4},{4,5},{5,6},{6,7},{7,0},{8,9},{9,10},{10,1... | collective-permute-start | bytes 2312 | tf_op jit(solution)/shard_map/ppermute | solution.py:124
  54.2 4.8 %collective-permute-start.7 = (bf16[1,3,128]{2,1,0:T(4,128)(2,1)S(1)}, bf16[1,3,128]{2,1,0:T(4,128)(2,1)S(1)}, u32[]{:S(2)}, u32[]{:S(2)}) collective-permute-start(bf16[1,3,128]{2,1,0:T(4,128)(2,1)S(1)} %collective-permute-done.6), channel_id=1, source_target_pairs={{0,1},{1,2},{2,3},{3,4},{4,5},{5,6},{6,7},{7,0},{8,9},{9,10},{10,1... | collective-permute-start | bytes 2312 | tf_op jit(solution)/shard_map/ppermute | solution.py:124
  59.0 4.8 %collective-permute-start.8 = (bf16[1,3,128]{2,1,0:T(4,128)(2,1)S(1)}, bf16[1,3,128]{2,1,0:T(4,128)(2,1)S(1)}, u32[]{:S(2)}, u32[]{:S(2)}) collective-permute-start(bf16[1,3,128]{2,1,0:T(4,128)(2,1)S(1)} %collective-permute-done.7), channel_id=1, source_target_pairs={{0,1},{1,2},{2,3},{3,4},{4,5},{5,6},{6,7},{7,0},{8,9},{9,10},{10,1... | collective-permute-start | bytes 2312 | tf_op jit(solution)/shard_map/ppermute | solution.py:124
  63.8 4.8 %collective-permute-start.9 = (bf16[1,3,128]{2,1,0:T(4,128)(2,1)S(1)}, bf16[1,3,128]{2,1,0:T(4,128)(2,1)S(1)}, u32[]{:S(2)}, u32[]{:S(2)}) collective-permute-start(bf16[1,3,128]{2,1,0:T(4,128)(2,1)S(1)} %collective-permute-done.8), channel_id=1, source_target_pairs={{0,1},{1,2},{2,3},{3,4},{4,5},{5,6},{6,7},{7,0},{8,9},{9,10},{10,1... | collective-permute-start | bytes 2312 | tf_op jit(solution)/shard_map/ppermute | solution.py:124
  68.6 4.8 %collective-permute-start.10 = (bf16[1,3,128]{2,1,0:T(4,128)(2,1)S(1)}, bf16[1,3,128]{2,1,0:T(4,128)(2,1)S(1)}, u32[]{:S(2)}, u32[]{:S(2)}) collective-permute-start(bf16[1,3,128]{2,1,0:T(4,128)(2,1)S(1)} %collective-permute-done.9), channel_id=1, source_target_pairs={{0,1},{1,2},{2,3},{3,4},{4,5},{5,6},{6,7},{7,0},{8,9},{9,10},{10,1... | collective-permute-start | bytes 2312 | tf_op jit(solution)/shard_map/ppermute | solution.py:124
  77.3 39.4 %copy-start.2 = (bf16[1,4,3,642]{3,1,2,0:T(4,128)(2,1)S(1)}, bf16[1,4,3,642]{3,1,2,0:T(4,128)(2,1)}, u32[]{:S(2)}) copy-start(bf16[1,4,3,642]{3,1,2,0:T(4,128)(2,1)} %param.24) | copy-start | bytes 46228
  115.1 3.6 %copy-start.3 = (bf16[1,4,3,642]{3,1,2,0:T(4,128)(2,1)S(1)}, bf16[1,4,3,642]{3,1,2,0:T(4,128)(2,1)}, u32[]{:S(2)}) copy-start(bf16[1,4,3,642]{3,1,2,0:T(4,128)(2,1)} %param.25) | copy-start | bytes 46228
  128.1 2.1 copy-start.1
  131.9 2.1 copy-start.1
  135.7 2.1 copy-start.1
  139.5 2.1 copy-start.1
  143.3 2.1 copy-start.1
  147.1 2.1 copy-start.1
  155.9 2.1 copy-start.1
  159.7 2.1 copy-start.1
  163.5 2.1 copy-start.1
  167.2 2.1 copy-start.1
  171.0 2.1 copy-start.1
  174.8 2.1 copy-start.1
  180.8 9.0 %all-to-all-start.1 = ((bf16[4,3,642]{2,1,0:T(4,128)(2,1)}), bf16[4,3,642]{2,1,0:T(4,128)(2,1)}, u32[]{:S(2)}, u32[]{:S(2)}) async-start(bf16[4,3,642]{2,1,0:T(4,128)(2,1)} %gather_fusion.5), calls=%async_computation.1 | async-start | bytes 49152 | tf_op jit(solution)/shard_map/all_to_all | solution.py:99
  189.8 43.1 %copy-start.5 = (f32[4]{0:T(128)S(1)}, f32[4]{0:T(128)}, u32[]{:S(2)}) copy-start(f32[4]{0:T(128)} %compare_convert_fusion) | copy-start | bytes 52
  189.8 44.0 %copy-start.4 = (s32[1,1,4]{2,1,0:T(1,128)S(1)}, s32[1,1,4]{2,1,0:T(1,128)}, u32[]{:S(2)}) copy-start(s32[1,1,4]{2,1,0:T(1,128)} %param.32) | copy-start | bytes 52
